TPU v7x, 256 devices: a whole 4x4x8 slice. The times are simulated.
256 devices in a mesh: frames: 16 (over z, core), mp: 16 (over y, x).
Axes of the slice: x: 4, y: 4, z: 8, core: 2. Of those that a mesh axis runs over, the one named last changes fastest.
Arguments:
- motion: bfloat16 [256, 25, 1024], P('frames', None, 'mp'), may hold values from -6 to 6
- adjacency: float32 [2, 25, 25], replicated, may hold values from -1.25 to 1.25
- w_bc: bfloat16 [2, 1024, 128], P(None, 'mp'), may hold values from -0.1875 to 0.1875
- decay: float32 [2, 256, 1024], P(None, 'frames', 'mp'), may hold values from 0.5 to 1, as said below
- skip: float32 [2, 1024], P(None, 'mp'), may hold values from 0.5 to 1.5
- w_out: bfloat16 [2, 1024, 1024], P(None, 'mp'), may hold values from -0.25 to 0.25
Outputs:
- encoded: float32 [256, 25, 1024], P('frames', None, 'mp')
Inputs may be any that keep to these rules, and one draw needn't show every extreme that they name: `decay`: each entry lies strictly between 0 and 1.
All inputs are finite; a program needn't handle non-finite values.
Results may differ from a plain program's by a relative error of at most 0.012.
Values may be sent and summed in bfloat16 or wider, within the bound.
A program may use at most 64 MiB of HBM per device.

v0:
```python
import jax
import jax.numpy as jnp
from jax import lax
from jax.sharding import PartitionSpec as P

ENCODER_LAYERS = 2


def entering(value, axis, join, neutral):
    count, mine = (lax.axis_size(axis), lax.axis_index(axis))
    pieces = jax.tree.map(lambda part: lax.all_gather(part, axis), value)
    so_far = jax.tree.map(
        lambda part, zero: jnp.full_like(part, 0) + jnp.asarray(zero, part.dtype), value, neutral
    )

    def lap(position, so_far):
        longer = join(so_far, jax.tree.map(lambda part: part[position], pieces))
        return jax.tree.map(lambda new, old: jnp.where(position < mine, new, old), longer, so_far)

    return lax.fori_loop(0, count - 1, lap, so_far)


def shards(motion, adjacency, w_bc, decay, skip, w_out):
    highest = lax.Precision.HIGHEST
    frames_loc, joints, width_loc = motion.shape
    state = w_bc.shape[2] // 2
    x = motion.astype(jnp.float32)
    for layer in range(ENCODER_LAYERS):
        mixed = jnp.einsum("jk,tkd->tjd", adjacency[layer], x, precision=highest).astype(
            jnp.bfloat16
        )
        partial_coef = jnp.dot(
            mixed.reshape(-1, width_loc), w_bc[layer], preferred_element_type=jnp.float32
        )
        coef = lax.psum(partial_coef, "mp").reshape(frames_loc, joints, 2 * state)
        in_b = coef[:, :, :state]
        out_c = coef[:, :, state:]
        decay_speed = decay[layer]
        logs = jnp.cumsum(jnp.log(decay_speed), axis=0)
        upto = jnp.exp(logs)
        weighted = (
            (1.0 - decay_speed)[:, None, :] * mixed.astype(jnp.float32) * jnp.exp(-logs)[:, None, :]
        )
        later = lax.broadcasted_iota(jnp.int32, (frames_loc, frames_loc), 0)
        earlier = lax.broadcasted_iota(jnp.int32, (frames_loc, frames_loc), 1)
        grid = jnp.einsum("tjn,sjn->jts", out_c, in_b, precision=highest)
        grid = jnp.where((earlier <= later)[None], grid, 0.0)
        inner = upto[:, None, :] * jnp.einsum("jts,sjd->tjd", grid, weighted, precision=highest)
        total = upto[-1]
        end_state = jnp.einsum(
            "sjd,sjn->jdn", weighted * total[None, None, :], in_b, precision=highest
        )

        def link(first, second):
            return (first[0] * second[0], second[0][None, :, None] * first[1] + second[1])

        _, incoming = entering(
            (total, end_state), "frames", link, (jnp.ones_like(total), jnp.zeros_like(end_state))
        )
        outer = upto[:, None, :] * jnp.einsum("tjn,jdn->tjd", out_c, incoming, precision=highest)
        result = (inner + outer + skip[layer][None, None, :] * mixed.astype(jnp.float32)).astype(
            jnp.bfloat16
        )
        flat = result.reshape(-1, width_loc)
        weights = w_out[layer]
        summed = lax.psum_scatter(
            lax.dot_general(
                weights, flat, (((0,), (1,)), ((), ())), preferred_element_type=jnp.float32
            ),
            "mp",
            scatter_dimension=0,
            tiled=True,
        )
        update = summed.T.reshape(frames_loc, joints, width_loc)
        x = x + update
    return x


def solution(mesh):
    return jax.shard_map(
        shards,
        mesh=mesh,
        in_specs=(
            P("frames", None, "mp"),
            P(),
            P(None, "mp", None),
            P(None, "frames", "mp"),
            P(None, "mp"),
            P(None, "mp", None),
        ),
        out_specs=P("frames", None, "mp"),
        check_vma=False,
    )
```

profile of v0, /device:TPU:32, one launch (start us, length us, event | category | flops | bytes accessed | tf_op | source)
XLA Modules:
  0.0 580.5 jit_solution(17792508891115939289)
XLA Ops:
  6.5 0.8 fusion.57
  7.4 1.2 fusion.36
  8.6 0.1 reshape.67
  8.7 0.9 fusion.53
  9.6 0.8 copy.58
  10.6 96.9 %all-reduce.3.cloned.1.call-done = f32[16,25,128]{2,0,1:T(8,128)} async-done(((f32[16,25,128]{2,0,1:T(8,128)}), f32[16,25,128]{2,0,1:T(8,128)}) %all-reduce.3.cloned.1.call-update) | async-done | bytes 204816 | tf_op jit(solution)/shard_map/psum | solution.py:35
  107.5 3.4 fusion.13
  111.0 15.9 %all-gather.2 = f32[16,1,64]{2,1,0:T(1,128)S(1)} all-gather(f32[1,1,64]{2,1,0:T(1,128)S(1)} %get-tuple-element.264), channel_id=1, replica_groups=mesh['frames'=16,'mp'=16] {'frames'}, dimensions={0}, use_global_device_ids=true | all-gather | bytes 4352 | tf_op jit(solution)/shard_map/all_gather | solution.py:11
  126.9 0.5 convolution_select_fusion.1
  127.5 58.7 %all-gather.7.cloned.1.call-done = f32[400,64,64]{2,1,0:T(8,128)} async-done(((f32[25,64,64]{2,1,0:T(8,128)}), f32[400,64,64]{2,1,0:T(8,128)}) %all-gather.7.cloned.1.call-update) | async-done | bytes 6553616 | tf_op jit(solution)/shard_map/all_gather | solution.py:11
  186.2 21.0 %while.28 = (s32[]{:T(128)}, f32[25,64,64]{2,1,0:T(8,128)S(1)}, s32[]{:T(128)}, f32[16,64]{1,0:T(8,128)S(1)}, f32[16,25,64,64]{3,2,1,0:T(8,128)}, /*index=5*/s32[]{:T(128)}, s32[]{:T(128)}) while((s32[]{:T(128)}, f32[25,64,64]{2,1,0:T(8,128)S(1)}, s32[]{:T(128)}, f32[16,64]{1,0:T(8,128)S(1)}, f32[16,25,64,64]{3,2,1,0:T(8,128)}, ...), condition=%wide.region_3.4_spmd.clone, body=%wide.region_2.3_spmd.clone.sunk | while | flops 409604 | bytes 1229673 | solution.py:20
  186.2 1.4 fusion.68
  187.6 1.4 fusion.68
  189.0 1.4 fusion.68
  190.4 1.4 fusion.68
  191.8 1.4 fusion.68
  193.2 1.4 fusion.68
  194.6 1.4 fusion.68
  196.0 1.4 fusion.68
  197.4 1.4 fusion.68
  198.8 1.4 fusion.68
  200.2 1.4 fusion.68
  201.6 1.4 fusion.68
  203.0 1.4 fusion.68
  204.4 1.4 fusion.68
  205.8 1.4 fusion.68
  207.2 1.4 fusion.27
  208.6 0.4 fusion.8
  209.1 0.3 convolution_bitcast_fusion.1
  209.5 1.8 copy.66
  211.4 79.9 %reduce-scatter.7.cloned.1.call-done = f32[64,400]{1,0:T(8,128)} async-done(((f32[1024,400]{1,0:T(8,128)}), f32[64,400]{1,0:T(8,128)}) %reduce-scatter.7.cloned.1.call-update) | async-done | bytes 102416
  291.3 1.0 copy.67
  292.3 0.4 fusion.31
  292.9 0.2 fusion.51
  293.1 0.8 copy.63
  294.0 94.0 %all-reduce.5.cloned.1.call-done = f32[16,25,128]{2,0,1:T(8,128)} async-done(((f32[16,25,128]{2,0,1:T(8,128)}), f32[16,25,128]{2,0,1:T(8,128)}) %all-reduce.5.cloned.1.call-update) | async-done | bytes 204816 | tf_op jit(solution)/shard_map/psum | solution.py:35
  387.9 3.4 fusion.18
  391.4 15.9 %all-gather.3 = f32[16,1,64]{2,1,0:T(1,128)S(1)} all-gather(f32[1,1,64]{2,1,0:T(1,128)S(1)} %get-tuple-element.260), channel_id=1, replica_groups=mesh['frames'=16,'mp'=16] {'frames'}, dimensions={0}, use_global_device_ids=true | all-gather | bytes 4352 | tf_op jit(solution)/shard_map/all_gather | solution.py:11
  407.3 0.5 convolution_select_fusion
  407.8 58.8 %all-gather.9.cloned.1.call-done = f32[400,64,64]{2,1,0:T(8,128)} async-done(((f32[25,64,64]{2,1,0:T(8,128)}), f32[400,64,64]{2,1,0:T(8,128)}) %all-gather.9.cloned.1.call-update) | async-done | bytes 6553616 | tf_op jit(solution)/shard_map/all_gather | solution.py:11
  466.6 21.0 %while.29 = (s32[]{:T(128)}, f32[25,64,64]{2,1,0:T(8,128)S(1)}, s32[]{:T(128)}, f32[16,64]{1,0:T(8,128)S(1)}, f32[16,25,64,64]{3,2,1,0:T(8,128)}, /*index=5*/s32[]{:T(128)}, s32[]{:T(128)}) while((s32[]{:T(128)}, f32[25,64,64]{2,1,0:T(8,128)S(1)}, s32[]{:T(128)}, f32[16,64]{1,0:T(8,128)S(1)}, f32[16,25,64,64]{3,2,1,0:T(8,128)}, ...), condition=%wide.region_8.9_spmd.clone, body=%wide.region_7.8_spmd.clone.sunk | while | flops 409604 | bytes 1229673 | solution.py:20
  466.6 1.4 fusion.69
  468.0 1.4 fusion.69
  469.4 1.4 fusion.69
  470.8 1.4 fusion.69
  472.2 1.4 fusion.69
  473.6 1.4 fusion.69
  475.0 1.4 fusion.69
  476.4 1.4 fusion.69
  477.8 1.4 fusion.69
  479.2 1.4 fusion.69
  480.6 1.4 fusion.69
  482.0 1.4 fusion.69
  483.4 1.4 fusion.69
  484.8 1.4 fusion.69
  486.2 1.4 fusion.69
  487.6 1.4 fusion.22
  489.0 0.4 fusion.9
  489.5 0.3 convolution_bitcast_fusion
  489.9 1.8 copy.68
  491.7 80.0 %reduce-scatter.9.cloned.1.call-done = f32[64,400]{1,0:T(8,128)} async-done(((f32[1024,400]{1,0:T(8,128)}), f32[64,400]{1,0:T(8,128)}) %reduce-scatter.9.cloned.1.call-update) | async-done | bytes 102416
  571.7 1.0 copy.69
  572.7 0.1 fusion.30
  572.8 0.8 copy.65
  (80 shorter events, 1.2 us)
Async XLA Ops:
  6.5 4.0 copy-start.5
  6.5 101.0 %all-reduce.3.cloned.1.call-start = ((), (), s32[]{:S(2)}) async-start(), calls=%async_computation.2 | async-start | bytes 409600 | tf_op jit(solution)/shard_map/psum | solution.py:35
  8.5 118.4 %copy-start.6 = (f32[2,64]{1,0:T(2,128)S(1)}, f32[2,64]{1,0:T(2,128)}, u32[]{:S(2)}) copy-start(f32[2,64]{1,0:T(2,128)} %param.14) | copy-start | bytes 1540
  10.5 175.7 %all-gather.7.cloned.1.call-start = ((), (), s32[]{:S(2)}) async-start(), calls=%async_computation.4 | async-start | bytes 13926400 | tf_op jit(solution)/shard_map/all_gather | solution.py:11
  107.5 19.4 %copy-start = (f32[16,25,128]{2,0,1:T(8,128)S(1)}, f32[16,25,128]{2,0,1:T(8,128)}, u32[]{:S(2)}) copy-start(f32[16,25,128]{2,0,1:T(8,128)} %all-reduce.3.cloned.1.call-done) | copy-start | bytes 614404
  110.9 180.3 %reduce-scatter.7.cloned.1.call-start = ((), (), s32[]{:S(2)}) async-start(), calls=%async_computation.6 | async-start | bytes 2228224
  207.2 1.9 copy-start.3
  211.3 81.0 %copy-start.2 = (bf16[16,25,64]{2,0,1:T(8,128)(2,1)S(1)}, bf16[16,25,64]{2,0,1:T(8,128)(2,1)}, u32[]{:S(2)}) copy-start(bf16[16,25,64]{2,0,1:T(8,128)(2,1)} %param.10) | copy-start | bytes 153604
  211.3 81.6 %copy-start.4 = (bf16[2,64,128]{2,1,0:T(8,128)(2,1)S(1)}, bf16[2,64,128]{2,1,0:T(8,128)(2,1)}, u32[]{:S(2)}) copy-start(bf16[2,64,128]{2,1,0:T(8,128)(2,1)} %param.12) | copy-start | bytes 98308
  211.3 176.6 %all-reduce.5.cloned.1.call-start = ((), (), s32[]{:S(2)}) async-start(), calls=%async_computation.3 | async-start | bytes 409600 | tf_op jit(solution)/shard_map/psum | solution.py:35
  293.9 172.7 %all-gather.9.cloned.1.call-start = ((), (), s32[]{:S(2)}) async-start(), calls=%async_computation.5 | async-start | bytes 13926400 | tf_op jit(solution)/shard_map/all_gather | solution.py:11
  387.9 19.4 %copy-start.1 = (f32[16,25,128]{2,0,1:T(8,128)S(1)}, f32[16,25,128]{2,0,1:T(8,128)}, u32[]{:S(2)}) copy-start(f32[16,25,128]{2,0,1:T(8,128)} %all-reduce.5.cloned.1.call-done) | copy-start | bytes 614404
  391.3 180.4 %reduce-scatter.9.cloned.1.call-start = ((), (), s32[]{:S(2)}) async-start(), calls=%async_computation.7 | async-start | bytes 2228224
Sparse Core Ops, SparseCore 0:
  10.6 96.8 all-reduce.2
  111.0 75.0 all-gather.6
  211.4 79.7 reduce-scatter.6
  294.3 93.5 all-reduce.4
  391.4 75.0 all-gather.8
  491.8 79.8 reduce-scatter.8
where the time goes:
time: 582 us; the launch traced here: 580 us
  waiting for transfers between devices  468 us (80%)
  other arithmetic  40.9 us (7%)
  blocking collectives  31.9 us (5%)
  matrix products  14.6 us (3%)
  between operations  13.8 us (2%)
  local copies, waits for them, and re-layouts  9.76 us (2%)
    psum x2, waiting for transfers between devices, shards(): coef = lax.psum(partial_coef, 'mp').reshape(frames_loc, joints, 2 * state)  191 us
    unnamed x8, waiting for transfers between devices  160 us
    all_gather x2, waiting for transfers between devices, entering(): pieces = jax.tree.map(lambda part: lax.all_gather(part, axis), value)  117 us
    select_n x30, other arithmetic, lap(): jnp.where(position < mine, new, old)  40.7 us
    all_gather x2, blocking collectives, entering(): pieces = jax.tree.map(lambda part: lax.all_gather(part, axis), value)  31.9 us
  transfers between devices with their start and end apart: 6, of which 6 were waited for; matrix products, arithmetic and copies ran while one was open for 0% of the time, Pallas kernels for 0%

commit v1 on v0

--- a/solution.py
+++ b/solution.py
@@ -32,7 +32,9 @@
         partial_coef = jnp.dot(
             mixed.reshape(-1, width_loc), w_bc[layer], preferred_element_type=jnp.float32
         )
-        coef = lax.psum(partial_coef, "mp").reshape(frames_loc, joints, 2 * state)
+        coef = jnp.sum(lax.all_gather(partial_coef, "mp"), axis=0).reshape(
+            frames_loc, joints, 2 * state
+        )
         in_b = coef[:, :, :state]
         out_c = coef[:, :, state:]
         decay_speed = decay[layer]

time: 582 us -> 502 us (0.86)
  waiting for transfers between devices: 468 us -> 385 us
    psum x2 -> x0, waiting for transfers between devices: 191 us -> none  [shards(): coef = lax.psum(partial_coef, 'mp').reshape(frames_loc, joints, 2 * state)]
    all_gather x0 -> x2, waiting for transfers between devices: none -> 108 us  [shards(): lax.all_gather(partial_coef, 'mp')]
where the time goes in v1:
time: 502 us; the launch traced here: 501 us
  waiting for transfers between devices  385 us (77%)
  other arithmetic  45.9 us (9%)
  blocking collectives  31.9 us (6%)
  matrix products  14.4 us (3%)
  between operations  13.8 us (3%)
  local copies, waits for them, and re-layouts  8.4 us (2%)
    unnamed x8, waiting for transfers between devices  160 us
    all_gather x2, waiting for transfers between devices, entering(): pieces = jax.tree.map(lambda part: lax.all_gather(part, axis), value)  117 us
    all_gather x2, waiting for transfers between devices, shards(): lax.all_gather(partial_coef, 'mp')  108 us
    select_n x30, other arithmetic, lap(): jnp.where(position < mine, new, old)  40.8 us
    all_gather x2, blocking collectives, entering(): pieces = jax.tree.map(lambda part: lax.all_gather(part, axis), value)  31.9 us
  transfers between devices with their start and end apart: 6, of which 6 were waited for; matrix products, arithmetic and copies ran while one was open for 0% of the time, Pallas kernels for 0%

profile of v1, /device:TPU:32, one launch (start us, length us, event | category | flops | bytes accessed | tf_op | source)
XLA Modules:
  0.0 500.7 jit_solution(2690077143369318330)
XLA Ops:
  6.5 0.8 fusion.59
  7.4 1.1 fusion.36
  8.7 1.6 fusion.53
  10.3 0.7 subtract_bitcast_fusion
  11.1 55.3 %all-gather.11.cloned.1.call-done = f32[6400,128]{1,0:T(8,128)} async-done(((f32[400,128]{1,0:T(8,128)}), f32[6400,128]{1,0:T(8,128)}) %all-gather.11.cloned.1.call-update) | async-done | bytes 3276816 | tf_op jit(solution)/shard_map/all_gather | solution.py:35
  66.5 2.1 reduce_sum.18
  68.6 0.1 fusion.58
  68.7 2.4 fusion.13
  71.2 15.9 %all-gather.4 = f32[16,1,64]{2,1,0:T(1,128)S(1)} all-gather(f32[1,1,64]{2,1,0:T(1,128)S(1)} %get-tuple-element.268), channel_id=1, replica_groups=mesh['frames'=16,'mp'=16] {'frames'}, dimensions={0}, use_global_device_ids=true | all-gather | bytes 4352 | tf_op jit(solution)/shard_map/all_gather | solution.py:11
  87.1 0.7 convolution_select_fusion.1
  87.8 58.5 %all-gather.13.cloned.1.call-done = f32[400,64,64]{2,1,0:T(8,128)} async-done(((f32[25,64,64]{2,1,0:T(8,128)}), f32[400,64,64]{2,1,0:T(8,128)}) %all-gather.13.cloned.1.call-update) | async-done | bytes 6553616 | tf_op jit(solution)/shard_map/all_gather | solution.py:11
  146.4 21.1 %while.28 = (s32[]{:T(128)}, f32[25,64,64]{2,1,0:T(8,128)S(1)}, s32[]{:T(128)}, f32[16,64]{1,0:T(8,128)S(1)}, f32[16,25,64,64]{3,2,1,0:T(8,128)}, /*index=5*/s32[]{:T(128)}, s32[]{:T(128)}) while((s32[]{:T(128)}, f32[25,64,64]{2,1,0:T(8,128)S(1)}, s32[]{:T(128)}, f32[16,64]{1,0:T(8,128)S(1)}, f32[16,25,64,64]{3,2,1,0:T(8,128)}, ...), condition=%wide.region_3.4_spmd.clone, body=%wide.region_2.3_spmd.clone.sunk | while | flops 409604 | bytes 1229673 | solution.py:20
  146.4 1.4 fusion.70
  147.8 1.4 fusion.70
  149.2 1.4 fusion.70
  150.6 1.4 fusion.70
  152.0 1.4 fusion.70
  153.4 1.4 fusion.70
  154.9 1.4 fusion.70
  156.3 1.4 fusion.70
  157.7 1.4 fusion.70
  159.1 1.4 fusion.70
  160.5 1.4 fusion.70
  161.9 1.4 fusion.70
  163.3 1.4 fusion.70
  164.7 1.4 fusion.70
  166.1 1.4 fusion.70
  167.5 1.4 fusion.29
  168.9 0.4 fusion.8
  169.4 0.3 convolution_bitcast_fusion.1
  169.7 1.8 copy.70
  171.6 79.9 %reduce-scatter.7.cloned.1.call-done = f32[64,400]{1,0:T(8,128)} async-done(((f32[1024,400]{1,0:T(8,128)}), f32[64,400]{1,0:T(8,128)}) %reduce-scatter.7.cloned.1.call-update) | async-done | bytes 102416
  251.5 1.0 copy.71
  252.6 0.4 fusion.21
  253.1 0.9 fusion.51
  254.1 52.8 %all-gather.15.cloned.1.call-done = f32[6400,128]{1,0:T(8,128)} async-done(((f32[400,128]{1,0:T(8,128)}), f32[6400,128]{1,0:T(8,128)}) %all-gather.15.cloned.1.call-update) | async-done | bytes 3276816 | tf_op jit(solution)/shard_map/all_gather | solution.py:35
  306.9 2.1 reduce_sum.19
  309.2 2.4 fusion.18
  311.6 15.9 %all-gather.5 = f32[16,1,64]{2,1,0:T(1,128)S(1)} all-gather(f32[1,1,64]{2,1,0:T(1,128)S(1)} %get-tuple-element.264), channel_id=1, replica_groups=mesh['frames'=16,'mp'=16] {'frames'}, dimensions={0}, use_global_device_ids=true | all-gather | bytes 4352 | tf_op jit(solution)/shard_map/all_gather | solution.py:11
  327.6 0.7 convolution_select_fusion
  328.2 58.6 %all-gather.17.cloned.1.call-done = f32[400,64,64]{2,1,0:T(8,128)} async-done(((f32[25,64,64]{2,1,0:T(8,128)}), f32[400,64,64]{2,1,0:T(8,128)}) %all-gather.17.cloned.1.call-update) | async-done | bytes 6553616 | tf_op jit(solution)/shard_map/all_gather | solution.py:11
  386.8 21.0 %while.29 = (s32[]{:T(128)}, f32[25,64,64]{2,1,0:T(8,128)S(1)}, s32[]{:T(128)}, f32[16,64]{1,0:T(8,128)S(1)}, f32[16,25,64,64]{3,2,1,0:T(8,128)}, /*index=5*/s32[]{:T(128)}, s32[]{:T(128)}) while((s32[]{:T(128)}, f32[25,64,64]{2,1,0:T(8,128)S(1)}, s32[]{:T(128)}, f32[16,64]{1,0:T(8,128)S(1)}, f32[16,25,64,64]{3,2,1,0:T(8,128)}, ...), condition=%wide.region_8.9_spmd.clone, body=%wide.region_7.8_spmd.clone.sunk | while | flops 409604 | bytes 1229673 | solution.py:20
  386.8 1.4 fusion.71
  388.2 1.4 fusion.71
  389.6 1.4 fusion.71
  391.0 1.4 fusion.71
  392.4 1.4 fusion.71
  393.8 1.4 fusion.71
  395.2 1.4 fusion.71
  396.6 1.4 fusion.71
  398.1 1.4 fusion.71
  399.5 1.4 fusion.71
  400.9 1.4 fusion.71
  402.3 1.4 fusion.71
  403.7 1.4 fusion.71
  405.1 1.4 fusion.71
  406.5 1.4 fusion.71
  407.8 1.4 fusion.24
  409.3 0.4 fusion.9
  409.7 0.4 convolution_bitcast_fusion
  410.1 1.8 copy.72
  411.9 80.0 %reduce-scatter.9.cloned.1.call-done = f32[64,400]{1,0:T(8,128)} async-done(((f32[1024,400]{1,0:T(8,128)}), f32[64,400]{1,0:T(8,128)}) %reduce-scatter.9.cloned.1.call-update) | async-done | bytes 102416
  491.9 1.0 copy.73
  493.0 0.8 copy.69
  (76 shorter events, 1.4 us)
Async XLA Ops:
  6.5 59.9 %all-gather.11.cloned.1.call-start = ((), (), s32[]{:S(2)}) async-start(), calls=%async_computation.2 | async-start | bytes 3481600 | tf_op jit(solution)/shard_map/all_gather | solution.py:35
  10.3 136.1 %all-gather.13.cloned.1.call-start = ((), (), s32[]{:S(2)}) async-start(), calls=%async_computation.3 | async-start | bytes 13926400 | tf_op jit(solution)/shard_map/all_gather | solution.py:11
  66.5 20.7 %copy-start.3 = (f32[2,64]{1,0:T(2,128)S(1)}, f32[2,64]{1,0:T(2,128)}, u32[]{:S(2)}) copy-start(f32[2,64]{1,0:T(2,128)} %param.14) | copy-start | bytes 1540
  71.1 180.4 %reduce-scatter.7.cloned.1.call-start = ((), (), s32[]{:S(2)}) async-start(), calls=%async_computation.6 | async-start | bytes 2228224
  146.4 23.0 %copy-start.1 = (bf16[2,64,1024]{2,1,0:T(8,128)(2,1)S(1)}, bf16[2,64,1024]{2,1,0:T(8,128)(2,1)}, u32[]{:S(2)}) copy-start(bf16[2,64,1024]{2,1,0:T(8,128)(2,1)} %param.15) | copy-start | bytes 786436
  169.7 82.8 %copy-start = (bf16[16,25,64]{2,0,1:T(8,128)(2,1)S(1)}, bf16[16,25,64]{2,0,1:T(8,128)(2,1)}, u32[]{:S(2)}) copy-start(bf16[16,25,64]{2,0,1:T(8,128)(2,1)} %param.10) | copy-start | bytes 153604
  169.7 83.4 %copy-start.2 = (bf16[2,64,128]{2,1,0:T(8,128)(2,1)S(1)}, bf16[2,64,128]{2,1,0:T(8,128)(2,1)}, u32[]{:S(2)}) copy-start(bf16[2,64,128]{2,1,0:T(8,128)(2,1)} %param.12) | copy-start | bytes 98308
  171.6 135.3 %all-gather.15.cloned.1.call-start = ((), (), s32[]{:S(2)}) async-start(), calls=%async_computation.4 | async-start | bytes 3481600 | tf_op jit(solution)/shard_map/all_gather | solution.py:35
  254.0 132.8 %all-gather.17.cloned.1.call-start = ((), (), s32[]{:S(2)}) async-start(), calls=%async_computation.5 | async-start | bytes 13926400 | tf_op jit(solution)/shard_map/all_gather | solution.py:11
  311.6 180.3 %reduce-scatter.9.cloned.1.call-start = ((), (), s32[]{:S(2)}) async-start(), calls=%async_computation.7 | async-start | bytes 2228224
Sparse Core Ops, SparseCore 0:
  10.4 56.0 all-gather.10
  71.2 75.0 all-gather.12
  171.7 79.7 reduce-scatter.6
  254.1 52.7 all-gather.14
  311.7 75.0 all-gather.16
  412.1 79.7 reduce-scatter.8
